TPU v7x, 128 devices: a whole 4x4x4 slice. The times are simulated.
128 devices in a mesh: row: 16 (over x, y_hi, core), col: 8 (over z, y_lo).
Axes of the slice: x: 4, y: 4 (y_hi: 2, y_lo: 2; y = y_hi * 2 + y_lo), z: 4, core: 2. Of those that a mesh axis runs over, the one named last changes fastest.
Arguments:
- a_vals: bfloat16 [512, 8, 64, 1024], P('row', 'col'), may hold values from -0.0625 to 0.0625
- a_cols: int32 [512, 8, 16], P('row', 'col'), may hold values from 0 to 63, all different within a row
- p_vals: bfloat16 [512, 64, 256], P(('row', 'col')), may hold values from -1.5 to 1.5
- p_cols: int32 [512, 4], P(('row', 'col')), may hold values from 0 to 15, all different within a row
Outputs:
- coarse_op: float32 [1024, 1024], P('row', 'col')
Inputs may be any that keep to these rules, and one draw needn't show every extreme that they name: `a_cols`: within one fine block row and column range the 16 entries are distinct. `p_cols`: within one fine block row the 4 entries are distinct.
All inputs are finite; a program needn't handle non-finite values.
Results may differ from a plain program's by a relative error of at most 0.0003.
Values may be sent and summed in bfloat16 or wider, within the bound.
No kernel may reach another device: no remote copies, remote signals or barrier semaphores. Data moves between devices by JAX's collectives and lax.ppermute only.
A program may use at most 128 MiB of HBM per device.

v0:
```python
import math
import jax
import jax.numpy as jnp
from jax import lax
from jax.sharding import PartitionSpec as P


def from_root(value, axis, source):
    kept = jnp.where(lax.axis_index(axis) == source, value, 0).astype(value.dtype)
    return lax.psum(kept, axis)


def contract_rows(p_slabs, p_kinds, wide, coarse):
    fine_rows = p_slabs.shape[0]
    block = p_slabs.shape[1]
    touched = p_kinds.shape[1]
    width = wide.shape[1]
    group = math.gcd(fine_rows, 4)
    slabs_g = p_slabs.reshape(fine_rows // group, group, block, touched * block)
    kinds_g = p_kinds.reshape(fine_rows // group, group, touched)
    wide_g = wide.reshape(fine_rows // group, group, block, width)

    def step(total, pieces):
        slab_part, kind_part, wide_part = pieces
        folded = jnp.einsum(
            "ire,irq->ieq",
            slab_part.astype(jnp.float32),
            wide_part,
            precision=lax.Precision.HIGHEST,
        )
        onehot = (kind_part[:, :, None] == lax.iota(jnp.int32, coarse)[None, None, :]).astype(
            jnp.float32
        )
        placed = jnp.einsum(
            "imn,imeq->neq",
            onehot,
            folded.reshape(group, touched, block, width),
            precision=lax.Precision.HIGHEST,
        )
        return (total + placed.reshape(coarse * block, width), None)

    start_total = jnp.zeros((coarse * block, width), jnp.float32)
    total, unused = lax.scan(step, start_total, (slabs_g, kinds_g, wide_g))
    return total


def shards(a_vals, a_cols, p_vals, p_cols):
    n_row = lax.axis_size("row")
    n_col = lax.axis_size("col")
    ratio = n_row // n_col
    block = a_vals.shape[2]
    per_row = a_cols.shape[2]
    touched = p_cols.shape[1]
    fine_rows = a_vals.shape[0]
    col_index = lax.axis_index("col")
    vals_r, ids_r = (
        lax.all_gather(p_vals, "col", axis=0, tiled=True),
        lax.all_gather(p_cols, "col", axis=0, tiled=True),
    )
    got_vals = []
    got_ids = []
    for offset in range(ratio):
        one_vals, one_ids = (
            from_root(vals_r, "row", ratio * col_index + offset),
            from_root(ids_r, "row", ratio * col_index + offset),
        )
        got_vals.append(one_vals)
        got_ids.append(one_ids)
    vals_c = jnp.concatenate(got_vals, axis=0)
    ids_c = jnp.concatenate(got_ids, axis=0)
    group = math.gcd(fine_rows, 4)
    tiles_a = a_vals[:, 0].reshape(fine_rows // group, group, block, per_row, block)
    where_a = a_cols[:, 0].reshape(fine_rows // group, group, per_row)

    def one_group(pair):
        tiles_part, where = pair
        flat_where = where.reshape(-1)
        picked = vals_c[flat_where].reshape(group, per_row, block, touched * block)
        kinds = ids_c[flat_where].reshape(group, per_row * touched)
        product = jnp.einsum(
            "irkf,ikfe->irke", tiles_part, picked, preferred_element_type=jnp.float32
        )
        product = product.reshape(group, block, per_row * touched, block)
        onehot = (kinds[:, :, None] == lax.iota(jnp.int32, n_row)[None, None, :]).astype(
            jnp.float32
        )
        placed = jnp.einsum("irsd,isn->irnd", product, onehot, precision=lax.Precision.HIGHEST)
        return placed.reshape(group * block, n_row * block)

    partial_w = lax.map(one_group, (tiles_a, where_a)).reshape(fine_rows * block, n_row * block)
    rows_out = n_row * block // n_row
    cols_out = n_row * block // n_col
    total = contract_rows(vals_r, ids_r, partial_w, n_row)
    total = total.reshape(n_row, rows_out, n_col, cols_out)
    total = jnp.transpose(total, (0, 2, 1, 3)).reshape(n_row * n_col * rows_out, cols_out)
    return lax.psum_scatter(total, ("row", "col"), scatter_dimension=0, tiled=True)


def solution(mesh):
    in_specs = (
        P("row", "col", None, None),
        P("row", "col", None),
        P(("row", "col"), None, None),
        P(("row", "col"), None),
    )
    out_specs = P("row", "col")
    return jax.shard_map(shards, mesh=mesh, in_specs=in_specs, out_specs=out_specs, check_vma=False)
```

profile of v0, /device:TPU:0, one launch (start us, length us, event | category | flops | bytes accessed | tf_op | source)
XLA Modules:
  0.0 1219.6 jit_solution(4784218886099866676)
XLA Ops:
  7.3 45.0 %all-gather.3.cloned.1.call-done = bf16[32,64,256]{2,1,0:T(8,128)(2,1)} async-done(((bf16[4,64,256]{2,1,0:T(8,128)(2,1)}), bf16[32,64,256]{2,1,0:T(8,128)(2,1)}) %all-gather.3.cloned.1.call-update) | async-done | bytes 1048592 | tf_op jit(solution)/shard_map/all_gather | solution.py:57
  55.1 24.8 %all-gather = s32[8,4,4]{2,1,0:T(4,128)S(1)} all-gather(s32[1,4,4]{2,1,0:T(4,128)S(1)} %bitcast.92), channel_id=1, replica_groups=mesh['row'=16,'col'=8] {'col'}, dimensions={0}, use_global_device_ids=true | all-gather | bytes 576 | tf_op jit(solution)/shard_map/all_gather | solution.py:58
  80.0 13.7 %all-reduce = (s32[32,4]{0,1:T(4,128)S(1)}, s32[32,4]{0,1:T(4,128)S(1)}) all-reduce(s32[32,4]{0,1:T(4,128)S(1)} %copy.32, s32[32,4]{0,1:T(4,128)S(1)} %copy.31), channel_id=1, replica_groups=mesh['row'=16,'col'=8] {'row'}, use_global_device_ids=true, to_apply=%region_3.4 | all-reduce | flops 256 | bytes 2048 | tf_op jit(solution)/shard_map/psum | solution.py:10
  93.9 11.6 reshape_squeeze.7
  105.6 94.5 %all-reduce.4.cloned.1.call-done = (bf16[32,64,256]{2,1,0:T(8,128)(2,1)}, bf16[32,64,256]{2,1,0:T(8,128)(2,1)}) async-done(((bf16[32,64,256]{2,1,0:T(8,128)(2,1)}, bf16[32,64,256]{2,1,0:T(8,128)(2,1)}), (bf16[32,64,256]{2,1,0:T(8,128)(2,1)}, bf16[32,64,256]{2,1,0:T(8,128)(2,1)})) %all-reduce.4.cloned.1.call-update) | async-done | bytes 2097168 | tf_op jit(solution)/shard_map/psum | solution.py:10
  203.2 186.4 %while.21 = (s32[]{:T(128)}, f32[8,256,1024]{2,1,0:T(8,128)}, s32[8,4,16]{2,1,0:T(4,128)S(1)}, s32[64,4]{1,0:T(8,128)S(1)}, bf16[64,64,256]{2,1,0:T(8,128)(2,1)}, /*index=5*/bf16[8,4,64,16,64]{4,3,2,1,0:T(8,128)(2,1)}, s32[]{:T(128)}) while((s32[]{:T(128)}, f32[8,256,1024]{2,1,0:T(8,128)}, s32[8,4,16]{2,1,0:T(4,128)S(1)}, ...), condition=%wide.region_5.6_spmd, body=%wide.region_4.5_spmd.sunk | while | flops 335549632 | bytes 38285140 | solution.py:90
  212.0 7.0 reshape.107
  235.4 7.0 reshape.107
  258.6 7.0 reshape.107
  281.9 7.0 reshape.107
  305.2 7.0 reshape.107
  328.6 7.0 reshape.107
  351.8 7.0 reshape.107
  375.1 7.0 reshape.107
  389.5 165.1 %while.22 = (s32[]{:T(128)}, f32[1024,1024]{1,0:T(8,128)}, s32[8,4,4]{2,1,0:T(4,128)S(1)}, bf16[8,4,64,256]{3,2,1,0:T(8,128)(2,1)}, f32[8,4,64,1024]{3,2,1,0:T(8,128)}, /*index=5*/s32[]{:T(128)}, s32[]{:T(128)}) while((s32[]{:T(128)}, f32[1024,1024]{1,0:T(8,128)}, s32[8,4,4]{2,1,0:T(4,128)S(1)}, bf16[8,4,64,256]{3,2,1,0:T(8,128)(2,1)}, ...), condition=%wide.region_7.8_spmd.clone, body=%wide.region_6.7_spmd.clone.sunk | while | flops 1008730368 | bytes 34735384 | solution.py:43
  392.7 6.4 fusion.39
  403.5 5.6 bitcast_add_fusion.2
  412.3 6.4 fusion.39
  423.0 6.9 bitcast_add_fusion.2
  433.1 6.4 fusion.39
  443.8 6.9 bitcast_add_fusion.2
  453.9 6.4 fusion.39
  464.6 6.9 bitcast_add_fusion.2
  474.7 6.4 fusion.39
  485.4 6.9 bitcast_add_fusion.2
  495.5 6.4 fusion.39
  506.2 6.9 bitcast_add_fusion.2
  516.3 6.4 fusion.39
  527.0 6.9 bitcast_add_fusion.2
  537.1 6.4 fusion.39
  547.8 6.9 bitcast_add_fusion.2
  560.6 652.5 %reduce-scatter.2.cloned.1.call-done = f32[64,128]{1,0:T(8,128)} async-done(((f32[8192,128]{1,0:T(8,128)}), f32[64,128]{1,0:T(8,128)}) %reduce-scatter.2.cloned.1.call-update) | async-done | bytes 32784 | tf_op jit(solution)/shard_map/reduce_scatter | solution.py:96
  (150 shorter events, 203.7 us)
Async XLA Ops:
  6.5 48.5 %copy-start.1 = (s32[4,4]{1,0:T(4,128)S(1)}, s32[4,4]{1,0:T(4,128)}, u32[]{:S(2)}) copy-start(s32[4,4]{1,0:T(4,128)} %param.11) | copy-start | bytes 196
  6.5 45.8 %all-gather.3.cloned.1.call-start = ((), (), s32[]{:S(2)}) async-start(), calls=%async_computation.1 | async-start | bytes 1179648 | tf_op jit(solution)/shard_map/all_gather | solution.py:57
  7.3 192.9 %all-reduce.4.cloned.1.call-start = ((), (), s32[]{:S(2)}) async-start(), calls=%async_computation.3 | async-start | bytes 4194304 | tf_op jit(solution)/shard_map/psum | solution.py:10
  55.0 1158.1 %reduce-scatter.2.cloned.1.call-start = ((), (), s32[]{:S(2)}) async-start(), calls=%async_computation.2 | async-start | bytes 4227072 | tf_op jit(solution)/shard_map/reduce_scatter | solution.py:96
  93.9 11.6 copy-start
Sparse Core Ops, SparseCore 0:
  9.0 43.3 all-gather.2
  55.1 144.9 all-reduce.3
  560.7 652.3 reduce-scatter.1
where the time goes:
time: 1220 us
  waiting for transfers between devices  793 us (65%)
  local copies, waits for them, and re-layouts  192 us (16%)
  matrix products  123 us (10%)
  other arithmetic  59.6 us (5%)
  blocking collectives  38.5 us (3%)
  between operations  13.2 us (1%)
    reduce_scatter x1, waiting for transfers between devices, shards(): lax.psum_scatter(total, ('row', 'col'), scatter_dimension=0, tiled=True)  653 us
    psum x1, waiting for transfers between devices, from_root(): return lax.psum(kept, axis)  94.5 us
    reshape x8, local copies, waits for them, and re-layouts, one_group(): product = product.reshape(group, block, per_row * touched, block)  55.7 us
    add x8, other arithmetic, step(): return (total + placed.reshape(coarse * block, width), None)  53.6 us
    dot_general x8, matrix products, step(): jnp.einsum('imn,imeq->neq', onehot, folded.reshape(group, touched, block,...  50.8 us
    all_gather x1, waiting for transfers between devices, shards(): lax.all_gather(p_vals, 'col', axis=0, tiled=True)  45 us
    dot_general x8, matrix products, one_group(): jnp.einsum('irsd,isn->irnd', product, onehot, precision=lax.Precision.HIG...  41.2 us
    dot_general x8, local copies, waits for them, and re-layouts, step(): jnp.einsum('imn,imeq->neq', onehot, folded.reshape(group, touched, block,...  35 us
  transfers between devices with their start and end apart: 3, of which 3 were waited for; matrix products, arithmetic and copies ran while one was open for 1% of the time, Pallas kernels for 0%

commit v1 on v0

--- a/solution.py
+++ b/solution.py
@@ -7,7 +7,7 @@
 
 def from_root(value, axis, source):
     kept = jnp.where(lax.axis_index(axis) == source, value, 0).astype(value.dtype)
-    return lax.psum(kept, axis)
+    return jnp.sum(lax.all_gather(kept, axis), axis=0)
 
 
 def contract_rows(p_slabs, p_kinds, wide, coarse):

time: 1220 us -> 1300 us (1.066)
  waiting for transfers between devices: 793 us -> 824 us
  blocking collectives: 38.5 us -> 69 us
  other arithmetic: 59.6 us -> 77.2 us
    all_gather x0 -> x2, waiting for transfers between devices: none -> 128 us  [from_root(): return jnp.sum(lax.all_gather(kept, axis), axis=0)]
    psum x1 -> x0, waiting for transfers between devices: 94.5 us -> none  [from_root(): return lax.psum(kept, axis)]
    all_gather x0 -> x2, blocking collectives: none -> 43.7 us  [from_root(): return jnp.sum(lax.all_gather(kept, axis), axis=0)]
    reduce_sum x0 -> x4, other arithmetic: none -> 18.6 us  [from_root(): return jnp.sum(lax.all_gather(kept, axis), axis=0)]
    psum x1 -> x0, blocking collectives: 13.7 us -> none  [from_root(): return lax.psum(kept, axis)]
  transfers between devices with their start and end apart: 3 -> 4, of which waited for: 3 -> 4; matrix products, arithmetic and copies ran while one was open for 1% -> 2% of each run, Pallas kernels for 0% -> 0%
where the time goes in v1:
time: 1300 us
  waiting for transfers between devices  824 us (63%)
  local copies, waits for them, and re-layouts  192 us (15%)
  matrix products  123 us (9%)
  other arithmetic  77.2 us (6%)
  blocking collectives  69 us (5%)
  between operations  13.2 us (1%)
    reduce_scatter x1, waiting for transfers between devices, shards(): lax.psum_scatter(total, ('row', 'col'), scatter_dimension=0, tiled=True)  650 us
    all_gather x2, waiting for transfers between devices, from_root(): return jnp.sum(lax.all_gather(kept, axis), axis=0)  128 us
    reshape x8, local copies, waits for them, and re-layouts, one_group(): product = product.reshape(group, block, per_row * touched, block)  55.6 us
    add x8, other arithmetic, step(): return (total + placed.reshape(coarse * block, width), None)  54.1 us
    dot_general x8, matrix products, step(): jnp.einsum('imn,imeq->neq', onehot, folded.reshape(group, touched, block,...  50.9 us
    all_gather x1, waiting for transfers between devices, shards(): lax.all_gather(p_vals, 'col', axis=0, tiled=True)  45 us
    all_gather x2, blocking collectives, from_root(): return jnp.sum(lax.all_gather(kept, axis), axis=0)  43.7 us
    dot_general x8, matrix products, one_group(): jnp.einsum('irsd,isn->irnd', product, onehot, precision=lax.Precision.HIG...  41.2 us
  transfers between devices with their start and end apart: 4, of which 4 were waited for; matrix products, arithmetic and copies ran while one was open for 2% of the time, Pallas kernels for 0%

profile of v1, /device:TPU:0, one launch (start us, length us, event | category | flops | bytes accessed | tf_op | source)
XLA Modules:
  0.0 1299.0 jit_solution(10629084319293644983)
XLA Ops:
  7.3 45.0 %all-gather.11.cloned.1.call-done = bf16[32,64,256]{2,1,0:T(8,128)(2,1)} async-done(((bf16[4,64,256]{2,1,0:T(8,128)(2,1)}), bf16[32,64,256]{2,1,0:T(8,128)(2,1)}) %all-gather.11.cloned.1.call-update) | async-done | bytes 1048592 | tf_op jit(solution)/shard_map/all_gather | solution.py:57
  55.8 25.2 %all-gather.4 = s32[8,4,4]{2,1,0:T(4,128)S(1)} all-gather(s32[1,4,4]{2,1,0:T(4,128)S(1)} %bitcast.96), channel_id=1, replica_groups=mesh['row'=16,'col'=8] {'col'}, dimensions={0}, use_global_device_ids=true | all-gather | bytes 576 | tf_op jit(solution)/shard_map/all_gather | solution.py:58
  81.2 24.1 %all-gather.5 = s32[16,32,4]{1,2,0:T(4,128)S(1)} all-gather(s32[1,32,4]{1,2,0:T(4,128)S(1)} %copy.29), channel_id=2, replica_groups=mesh['row'=16,'col'=8] {'row'}, dimensions={0}, use_global_device_ids=true | all-gather | bytes 8704 | tf_op jit(solution)/shard_map/all_gather | solution.py:10
  105.4 19.6 %all-gather.6 = s32[16,32,4]{1,2,0:T(4,128)S(1)} all-gather(s32[1,32,4]{1,2,0:T(4,128)S(1)} %copy.30), channel_id=3, replica_groups=mesh['row'=16,'col'=8] {'row'}, dimensions={0}, use_global_device_ids=true | all-gather | bytes 8704 | tf_op jit(solution)/shard_map/all_gather | solution.py:10
  125.2 11.6 reshape_squeeze.7
  136.9 27.3 %all-gather.13.cloned.1.call-done = bf16[512,64,256]{2,1,0:T(8,128)(2,1)} async-done(((bf16[32,64,256]{2,1,0:T(8,128)(2,1)}), bf16[512,64,256]{2,1,0:T(8,128)(2,1)}) %all-gather.13.cloned.1.call-update) | async-done | bytes 16777232 | tf_op jit(solution)/shard_map/all_gather | solution.py:10
  164.1 9.3 reduce_sum.44
  173.4 100.6 %all-gather.15.cloned.1.call-done = bf16[512,64,256]{2,1,0:T(8,128)(2,1)} async-done(((bf16[32,64,256]{2,1,0:T(8,128)(2,1)}), bf16[512,64,256]{2,1,0:T(8,128)(2,1)}) %all-gather.15.cloned.1.call-update) | async-done | bytes 16777232 | tf_op jit(solution)/shard_map/all_gather | solution.py:10
  274.0 9.3 reduce_sum.45
  284.8 186.4 %while.21 = (s32[]{:T(128)}, f32[8,256,1024]{2,1,0:T(8,128)}, s32[8,4,16]{2,1,0:T(4,128)S(1)}, s32[64,4]{1,0:T(8,128)S(1)}, bf16[64,64,256]{2,1,0:T(8,128)(2,1)}, /*index=5*/bf16[8,4,64,16,64]{4,3,2,1,0:T(8,128)(2,1)}, s32[]{:T(128)}) while((s32[]{:T(128)}, f32[8,256,1024]{2,1,0:T(8,128)}, s32[8,4,16]{2,1,0:T(4,128)S(1)}, ...), condition=%wide.region_5.6_spmd, body=%wide.region_4.5_spmd.sunk | while | flops 335549632 | bytes 38285140 | solution.py:90
  293.7 6.9 reshape.119
  316.9 6.9 reshape.119
  340.3 6.9 reshape.119
  363.6 6.9 reshape.119
  386.9 6.9 reshape.119
  410.1 6.9 reshape.119
  433.5 6.9 reshape.119
  456.8 6.9 reshape.119
  471.2 165.6 %while.22 = (s32[]{:T(128)}, f32[1024,1024]{1,0:T(8,128)}, s32[8,4,4]{2,1,0:T(4,128)S(1)}, bf16[8,4,64,256]{3,2,1,0:T(8,128)(2,1)}, f32[8,4,64,1024]{3,2,1,0:T(8,128)}, /*index=5*/s32[]{:T(128)}, s32[]{:T(128)}) while((s32[]{:T(128)}, f32[1024,1024]{1,0:T(8,128)}, s32[8,4,4]{2,1,0:T(4,128)S(1)}, bf16[8,4,64,256]{3,2,1,0:T(8,128)(2,1)}, ...), condition=%wide.region_7.8_spmd.clone, body=%wide.region_6.7_spmd.clone.sunk | while | flops 1008730368 | bytes 34735384 | solution.py:43
  504.7 6.9 bitcast_add_fusion.2
  514.8 6.4 fusion.39
  525.6 6.9 bitcast_add_fusion.2
  535.7 6.4 fusion.39
  546.4 6.9 bitcast_add_fusion.2
  556.6 6.4 fusion.39
  567.3 6.9 bitcast_add_fusion.2
  577.4 6.4 fusion.39
  588.2 6.9 bitcast_add_fusion.2
  598.3 6.4 fusion.39
  609.0 6.9 bitcast_add_fusion.2
  629.9 6.9 bitcast_add_fusion.2
  642.7 649.7 %reduce-scatter.2.cloned.1.call-done = f32[64,128]{1,0:T(8,128)} async-done(((f32[8192,128]{1,0:T(8,128)}), f32[64,128]{1,0:T(8,128)}) %reduce-scatter.2.cloned.1.call-update) | async-done | bytes 32784 | tf_op jit(solution)/shard_map/reduce_scatter | solution.py:96
  (158 shorter events, 227.8 us)
Async XLA Ops:
  6.5 49.3 %copy-start.1 = (s32[4,4]{1,0:T(4,128)S(1)}, s32[4,4]{1,0:T(4,128)}, u32[]{:S(2)}) copy-start(s32[4,4]{1,0:T(4,128)} %param.11) | copy-start | bytes 196
  6.5 45.8 %all-gather.11.cloned.1.call-start = ((), (), s32[]{:S(2)}) async-start(), calls=%async_computation.1 | async-start | bytes 1179648 | tf_op jit(solution)/shard_map/all_gather | solution.py:57
  7.3 156.9 %all-gather.13.cloned.1.call-start = ((), (), s32[]{:S(2)}) async-start(), calls=%async_computation.3 | async-start | bytes 17825792 | tf_op jit(solution)/shard_map/all_gather | solution.py:10
  55.0 219.0 %all-gather.15.cloned.1.call-start = ((), (), s32[]{:S(2)}) async-start(), calls=%async_computation.4 | async-start | bytes 17825792 | tf_op jit(solution)/shard_map/all_gather | solution.py:10
  55.8 1236.7 %reduce-scatter.2.cloned.1.call-start = ((), (), s32[]{:S(2)}) async-start(), calls=%async_computation.2 | async-start | bytes 4227072 | tf_op jit(solution)/shard_map/reduce_scatter | solution.py:96
  125.2 11.6 copy-start
Sparse Core Ops, SparseCore 0:
  9.0 43.3 all-gather.10
  55.1 108.9 all-gather.12
  166.5 107.4 all-gather.14
  642.8 649.5 reduce-scatter.1
